TPU v7x, 32 devices: a whole 2x2x4 slice. The times are simulated.
32 devices in a mesh: band: 4 (over y, x), pair: 8 (over z, core).
Axes of the slice: x: 2, y: 2, z: 4, core: 2. Of those that a mesh axis runs over, the one named last changes fastest.
Arguments:
- visibilities: float32 [4, 16, 8, 2, 1024], P('band', 'pair'), may hold values from -6 to 6
- coherencies: bfloat16 [4, 16, 8, 2, 32, 1024], P('band', 'pair'), may hold values from -1 to 1
- block_tiles: int32 [16, 2], P('pair'), may hold values from 0 to 15, as said below
- sample_counts: int32 [16], P('pair'), may hold values from 1 to 8, as said below
- gains: float32 [4, 2, 32, 512], P('band', None, None, 'pair'), may hold values from 0.5 to 1.5
- targets: float32 [4, 2, 32, 512], P('band', None, None, 'pair'), may hold values from 0.5 to 1.5
- multipliers: float32 [4, 2, 32, 512], P('band', None, None, 'pair'), may hold values from -2 to 2
Outputs:
- new_gains: float32 [4, 2, 32, 512], P('band', None, None, 'pair')
- new_targets: float32 [4, 2, 32, 512], P('band', None, None, 'pair')
- new_multipliers: float32 [4, 2, 32, 512], P('band', None, None, 'pair')
Inputs may be any that keep to these rules, and one draw needn't show every extreme that they name: `block_tiles`: each row names two station tiles a <= b; no tile pair appears twice; the pairs (0, 15) and (15, 15) are always among them. `sample_counts`: some block has all 8 samples and some block only one.
All inputs are finite; a program needn't handle non-finite values.
Results may differ from a plain program's by a relative error of at most 0.0003.
Values sent between devices are 32-bit elements; how exact they have to be, the bound alone decides.
No kernel may reach another device: no remote copies, remote signals or barrier semaphores. Data moves between devices by JAX's collectives and lax.ppermute only.
A program may use at most 64 MiB of HBM per device.

v0:
```python
import math
import jax
import jax.numpy as jnp
from jax import lax
from jax.sharding import PartitionSpec as P

K = 32
P_SIZE = 8
TILE = 32
ITERS = 2
TIMES = 8
ridge = 0.05
penalty = 0.25


def bernstein_table(freq_count, term_count):
    positions = (jnp.arange(freq_count).astype(jnp.float32) + 0.5) / freq_count
    columns = [
        math.comb(term_count - 1, degree)
        * positions**degree
        * (1.0 - positions) ** (term_count - 1 - degree)
        for degree in range(term_count)
    ]
    return jnp.stack(columns, axis=1)


def block_terms(gains_first, gains_second, vis_block, coh_block, same_tile, valid_count):
    tile_width = gains_first.shape[-1]
    left_gains = jnp.repeat(gains_first, tile_width, axis=-1)
    right_gains = jnp.tile(gains_second, (1, 1, tile_width))
    prod_real = left_gains[0] * right_gains[0] + left_gains[1] * right_gains[1]
    prod_imag = left_gains[1] * right_gains[0] - left_gains[0] * right_gains[1]
    cohere = coh_block.astype(jnp.float32)
    coh_real = cohere[:, 0]
    coh_imag = cohere[:, 1]
    model_real = jnp.sum(prod_real[None] * coh_real - prod_imag[None] * coh_imag, axis=1)
    model_imag = jnp.sum(prod_real[None] * coh_imag + prod_imag[None] * coh_real, axis=1)
    sample_total = vis_block.shape[0]
    cell_index = jnp.arange(tile_width * tile_width)
    row_index = cell_index // tile_width
    col_index = cell_index % tile_width
    keep_cell = (row_index < col_index) | jnp.logical_not(same_tile)
    keep_time = jnp.arange(sample_total) < valid_count
    weight = (keep_time[:, None] & keep_cell[None, :]).astype(jnp.float32)
    res_real = (vis_block[:, 0] - model_real) * weight
    res_imag = (vis_block[:, 1] - model_imag) * weight
    acc_real = jnp.sum(res_real[:, None] * coh_real + res_imag[:, None] * coh_imag, axis=0)
    acc_imag = jnp.sum(res_imag[:, None] * coh_real - res_real[:, None] * coh_imag, axis=0)
    term_real = acc_real * right_gains[0] - acc_imag * right_gains[1]
    term_imag = acc_real * right_gains[1] + acc_imag * right_gains[0]
    direction_count = acc_real.shape[0]
    grad_first = (
        -jnp.stack([term_real, term_imag])
        .reshape(2, direction_count, tile_width, tile_width)
        .sum(axis=3)
    )
    other_real = acc_real * left_gains[0] + acc_imag * left_gains[1]
    other_imag = acc_real * left_gains[1] - acc_imag * left_gains[0]
    grad_second = (
        -jnp.stack([other_real, other_imag])
        .reshape(2, direction_count, tile_width, tile_width)
        .sum(axis=2)
    )
    return (grad_first, grad_second)


def data_gradient(gain_band, vis_band, coh_band, block_tiles, sample_counts):
    direction_count = gain_band.shape[1]
    station_count = gain_band.shape[2]
    tile_count = station_count // TILE
    tile_range = jnp.arange(tile_count)
    onehot_first = (block_tiles[:, 0:1] == tile_range[None, :]).astype(jnp.float32)
    onehot_second = (block_tiles[:, 1:2] == tile_range[None, :]).astype(jnp.float32)
    grid = gain_band.reshape(2, direction_count, tile_count, TILE)
    tiles_first = jnp.einsum("bn,cknt->bckt", onehot_first, grid, precision=lax.Precision.HIGHEST)
    tiles_second = jnp.einsum("bn,cknt->bckt", onehot_second, grid, precision=lax.Precision.HIGHEST)
    same_tile = block_tiles[:, 0] == block_tiles[:, 1]
    grad_first, grad_second = jax.vmap(block_terms)(
        tiles_first, tiles_second, vis_band, coh_band, same_tile, sample_counts
    )
    total = jnp.einsum("bn,bckt->cknt", onehot_first, grad_first, precision=lax.Precision.HIGHEST)
    total = total + jnp.einsum(
        "bn,bckt->cknt", onehot_second, grad_second, precision=lax.Precision.HIGHEST
    )
    return total.reshape(2, direction_count, station_count)


def local(visibilities, coherencies, block_tiles, sample_counts, gains, targets, multipliers):
    pair_count = lax.axis_size("pair")
    band_count = lax.axis_size("band")
    station_local = gains.shape[3]
    block_total = block_tiles.shape[0] * pair_count
    tile_count = station_local * pair_count // TILE
    step_size = 0.25 * tile_count * K / (TIMES * TILE * block_total)
    current = gains
    for iteration in range(ITERS):
        whole_gains = lax.all_gather(current, "pair", axis=3, tiled=True)
        partial_value = jax.vmap(data_gradient, in_axes=(0, 0, 0, None, None))(
            whole_gains, visibilities, coherencies, block_tiles, sample_counts
        )
        summed = lax.psum_scatter(partial_value, "pair", scatter_dimension=3, tiled=True)
        current = current - step_size * summed - penalty * (current - targets + multipliers)
    freq_local = gains.shape[0]
    freq_total = freq_local * band_count
    basis_table = bernstein_table(freq_total, P_SIZE)
    normal = jnp.dot(basis_table.T, basis_table, precision=lax.Precision.HIGHEST) + ridge * jnp.eye(
        P_SIZE, dtype=jnp.float32
    )
    factor = jnp.linalg.cholesky(normal)
    flattened = (current + multipliers).reshape(freq_local, -1)
    own_basis = lax.dynamic_slice_in_dim(
        basis_table, lax.axis_index("band") * freq_local, freq_local, 0
    )
    all_bands = lax.all_gather(flattened, "band", axis=0, tiled=True)
    moments = jnp.dot(basis_table.T, all_bands, precision=lax.Precision.HIGHEST)
    coeffs = jax.scipy.linalg.cho_solve((factor, True), moments)
    fitted = jnp.dot(own_basis, coeffs, precision=lax.Precision.HIGHEST).reshape(current.shape)
    return (current, fitted, multipliers + current - fitted)


def solution(mesh):
    placed = (
        P("band", "pair", None, None, None),
        P("band", "pair", None, None, None, None),
        P("pair", None),
        P("pair"),
        P("band", None, None, "pair"),
        P("band", None, None, "pair"),
        P("band", None, None, "pair"),
    )
    return jax.shard_map(
        local,
        mesh=mesh,
        in_specs=placed,
        out_specs=(
            P("band", None, None, "pair"),
            P("band", None, None, "pair"),
            P("band", None, None, "pair"),
        ),
        check_vma=False,
    )
```

profile of v0, /device:TPU:0, one launch (start us, length us, event | category | flops | bytes accessed | tf_op | source)
XLA Modules:
  0.0 149.3 jit_solution(11101035761976110209)
XLA Ops:
  7.2 1.0 slice_reduce_fusion.1
  8.2 0.9 not_reduce_fusion
  9.1 0.9 copy.27
  10.0 16.5 %all_gather.9 = f32[1,2,32,512]{2,1,0,3:T(2,128)S(1)} all-gather(f32[1,2,32,64]{2,1,0,3:T(2,128)S(1)} %copy.27), channel_id=1, replica_groups=mesh['band'=4,'pair'=8] {'pair'}, dimensions={3}, use_global_device_ids=true | all-gather | bytes 147456 | tf_op jit(solution)/shard_map/all_gather | solution.py:97
  27.1 0.6 broadcast_in_dim.9
  27.7 1.0 broadcast_in_dim.10
  29.2 1.0 tile.9
  30.1 2.1 %convert_element_type.71 = f32[1,2,8,2,32,1024]{5,4,3,2,1,0:T(8,128)S(1)} convert(bf16[1,2,8,2,32,1024]{5,4,3,2,1,0:T(8,128)(2,1)} %param.8) | non-fusion elementwise | flops 1048576 | bytes 6291456 | tf_op jit(solution)/shard_map/vmap(vmap())/convert_element_type | solution.py:33
  32.6 0.8 subtract_reduce_fusion.3
  33.5 0.7 copy-done
  34.2 0.6 add_reduce_fusion.2
  35.1 0.7 reshape.953
  35.8 0.6 reduce_sum.132
  36.4 0.5 fusion.31
  36.9 0.7 reshape.954
  37.6 0.4 reduce_sum.133
  38.1 0.5 fusion.1
  38.6 0.3 copy.60
  38.9 1.0 reshape.971
  40.4 0.7 cholesky.16
  41.2 30.8 %reduce-scatter.7.cloned.1.call-done = f32[64,64]{1,0:T(8,128)} async-done(((f32[512,64]{1,0:T(8,128)}), f32[64,64]{1,0:T(8,128)}) %reduce-scatter.7.cloned.1.call-update) | async-done | bytes 16400
  72.0 0.9 reshape.972
  73.1 15.1 %all_gather.10 = f32[1,2,32,512]{2,1,0,3:T(2,128)S(1)} all-gather(f32[1,2,32,64]{2,1,0,3:T(2,128)S(1)} %copy.35), channel_id=1, replica_groups=mesh['band'=4,'pair'=8] {'pair'}, dimensions={3}, use_global_device_ids=true | all-gather | bytes 147456 | tf_op jit(solution)/shard_map/all_gather | solution.py:97
  88.8 0.3 fusion.63
  89.1 0.6 broadcast_in_dim.11
  89.7 1.0 broadcast_in_dim.12
  90.9 1.0 tile.21
  91.9 3.2 %subtract_reduce_fusion.1 = (f32[2,8,1024]{2,1,0:T(8,128)S(1)}, f32[2,8,1024]{2,1,0:T(8,128)S(1)}) fusion(f32[1,2,8,2,32,1024]{5,4,3,2,1,0:T(8,128)} %copy-done, f32[2,32,1024]{2,1,0:T(8,128)S(1)} %get-tuple-element.20, f32[2,32,1024]{2,1,0:T(8,128)S(1)} %get-tuple-element.19), kind=kLoop, calls=%fused_computation.5 | loop fusion | flops 4161536 | bytes 4849664 | tf_op jit(solution)/shard_map/vmap(vmap())/reduce_sum | solution.py:36
  95.3 0.6 add_reduce_fusion
  96.2 0.7 reshape.958
  96.9 0.4 reduce_sum.143
  97.4 0.7 reshape.957
  98.1 0.6 reduce_sum.142
  98.7 0.5 fusion.28
  99.2 0.5 fusion
  99.7 0.3 copy.61
  100.0 1.0 reshape.973
  101.1 0.6 compare_reduce_fusion
  101.7 0.6 fusion.39
  102.4 0.6 custom-call.10
  103.0 27.3 %reduce-scatter.9.cloned.1.call-done = f32[64,64]{1,0:T(8,128)} async-done(((f32[512,64]{1,0:T(8,128)}), f32[64,64]{1,0:T(8,128)}) %reduce-scatter.9.cloned.1.call-update) | async-done | bytes 16400
  130.2 0.9 reshape.974
  131.2 0.6 fusion.80
  131.9 8.2 %all-gather = f32[4,1,4096]{2,1,0:T(1,128)S(1)} all-gather(f32[1,1,4096]{2,1,0:T(1,128)S(1)} %reshape.962), channel_id=1, replica_groups=mesh['band'=4,'pair'=8] {'band'}, dimensions={0}, use_global_device_ids=true | all-gather | bytes 81920 | tf_op jit(solution)/shard_map/all_gather | solution.py:114
  140.6 0.5 fusion.18
  141.1 0.3 fusion.42
  141.4 0.4 fusion.68
  141.8 0.6 sub.231
  (63 shorter events, 4.5 us)
Async XLA Ops:
  7.2 64.8 %reduce-scatter.7.cloned.1.call-start = ((), (), s32[]{:S(2)}) async-start(), calls=%async_computation.2 | async-start | bytes 294912
  30.1 2.1 %copy-start.4 = (f32[1,2,8,2,1024]{4,3,2,1,0:T(2,128)S(1)}, f32[1,2,8,2,1024]{4,3,2,1,0:T(2,128)}, u32[]{:S(2)}) copy-start(f32[1,2,8,2,1024]{4,3,2,1,0:T(2,128)} %param.7) | copy-start | bytes 393220
  30.1 2.2 %copy-start.7 = (s32[2]{0:T(128)S(1)}, s32[2]{0:T(128)}, u32[]{:S(2)}) copy-start(s32[2]{0:T(128)} %param.10) | copy-start | bytes 28
  32.2 1.9 %copy-start = (f32[1,2,8,2,32,1024]{5,4,3,2,1,0:T(8,128)}, f32[1,2,8,2,32,1024]{5,4,3,2,1,0:T(8,128)S(1)}, u32[]{:S(2)}) copy-start(f32[1,2,8,2,32,1024]{5,4,3,2,1,0:T(8,128)S(1)} %convert_element_type.71) | copy-start | bytes 12582916
  38.0 34.9 %copy-start.2 = (f32[1,2,32,64]{3,2,1,0:T(8,128)S(1)}, f32[1,2,32,64]{3,2,1,0:T(8,128)}, u32[]{:S(2)}) copy-start(f32[1,2,32,64]{3,2,1,0:T(8,128)} %param.11) | copy-start | bytes 49156
  38.1 34.9 %copy-start.5 = (f32[1,2,32,64]{3,2,1,0:T(8,128)S(1)}, f32[1,2,32,64]{3,2,1,0:T(8,128)}, u32[]{:S(2)}) copy-start(f32[1,2,32,64]{3,2,1,0:T(8,128)} %param.13) | copy-start | bytes 49156
  38.1 34.9 %copy-start.6 = (f32[1,2,32,64]{3,2,1,0:T(8,128)S(1)}, f32[1,2,32,64]{3,2,1,0:T(8,128)}, u32[]{:S(2)}) copy-start(f32[1,2,32,64]{3,2,1,0:T(8,128)} %param.12) | copy-start | bytes 49156
  39.9 90.3 %reduce-scatter.9.cloned.1.call-start = ((), (), s32[]{:S(2)}) async-start(), calls=%async_computation.3 | async-start | bytes 294912
  91.9 3.5 %copy-start.1 = (f32[1,2,8,2,32,1024]{5,4,3,2,1,0:T(8,128)S(1)}, f32[1,2,8,2,32,1024]{5,4,3,2,1,0:T(8,128)}, u32[]{:S(2)}) copy-start(f32[1,2,8,2,32,1024]{5,4,3,2,1,0:T(8,128)} %copy-done) | copy-start | bytes 12582916
  141.8 0.6 copy-start.3
Sparse Core Ops, SparseCore 0:
  40.1 31.8 reduce-scatter.6
  101.2 29.0 reduce-scatter.8
where the time goes:
time: 150 us; the launch traced here: 149 us
  waiting for transfers between devices  58.1 us (39%)
  blocking collectives  39.9 us (27%)
  local copies, waits for them, and re-layouts  16.4 us (11%)
  other arithmetic  15.4 us (10%)
  between operations  14.5 us (10%)
  matrix products  4.94 us (3%)
    unnamed x4, waiting for transfers between devices  58.1 us
    all_gather x2, blocking collectives, local(): whole_gains = lax.all_gather(current, 'pair', axis=3, tiled=True)  31.6 us
    all_gather x1, blocking collectives, local(): all_bands = lax.all_gather(flattened, 'band', axis=0, tiled=True)  8.23 us
    unnamed x26, local copies, waits for them, and re-layouts  6.34 us
    reduce_sum x2, other arithmetic, block_terms(): jnp.sum(prod_real[None] * coh_real - prod_imag[None] * coh_imag, axis=1)  3.97 us
    broadcast_in_dim x4, local copies, waits for them, and re-layouts, block_terms(): left_gains = jnp.repeat(gains_first, tile_width, axis=-1)  3.11 us
  transfers between devices with their start and end apart: 2, of which 2 were waited for; matrix products, arithmetic and copies ran while one was open for 2% of the time, Pallas kernels for 0%

commit v1 on v0

--- a/solution.py
+++ b/solution.py
@@ -11,6 +11,18 @@
 TIMES = 8
 ridge = 0.05
 penalty = 0.25
+
+
+def collect(x, axis, dim):
+    ways, here = (lax.axis_size(axis), lax.axis_index(axis))
+    grown, reach = (x, 1)
+    while reach < ways:
+        theirs = lax.ppermute(grown, axis, [(d, d ^ reach) for d in range(ways)])
+        mine_first = jnp.concatenate([grown, theirs], axis=dim)
+        theirs_first = jnp.concatenate([theirs, grown], axis=dim)
+        grown = jnp.where(here & reach == 0, mine_first, theirs_first)
+        reach = 2 * reach
+    return grown
 
 
 def bernstein_table(freq_count, term_count):
@@ -94,7 +106,7 @@
     step_size = 0.25 * tile_count * K / (TIMES * TILE * block_total)
     current = gains
     for iteration in range(ITERS):
-        whole_gains = lax.all_gather(current, "pair", axis=3, tiled=True)
+        whole_gains = collect(current, "pair", 3)
         partial_value = jax.vmap(data_gradient, in_axes=(0, 0, 0, None, None))(
             whole_gains, visibilities, coherencies, block_tiles, sample_counts
         )

time: 150 us -> 147 us (0.980)
  blocking collectives: 39.9 us -> 8.28 us
  waiting for transfers between devices: 58.1 us -> 72.9 us
  starting transfers between devices: 0.08 us -> 6.63 us
  other arithmetic: 15.4 us -> 21.9 us
    all_gather x2 -> x0, blocking collectives: 31.6 us -> none  [local(): whole_gains = lax.all_gather(current, 'pair', axis=3, tiled=True)]
    ppermute x0 -> x6, waiting for transfers between devices: none -> 13.8 us  [collect(): theirs = lax.ppermute(grown, axis, [(d, d ^ reach) for d in range(ways)])]
    ppermute x0 -> x6, starting transfers between devices: none -> 6.37 us  [collect(): theirs = lax.ppermute(grown, axis, [(d, d ^ reach) for d in range(ways)])]
    reduce_sum x2, other arithmetic: 3.97 us -> 6.35 us  [block_terms(): jnp.sum(prod_real[None] * coh_real - prod_imag[None] * coh_imag, axis=1)]
    convert_element_type x1, other arithmetic: 2.07 us -> 4.01 us  [block_terms(): cohere = coh_block.astype(jnp.float32)]
    concatenate x0 -> x8, local copies, waits for them, and re-layouts: none -> 1.58 us  [collect(): mine_first = jnp.concatenate([grown, theirs], axis=dim)]
    unnamed x26 -> x23, local copies, waits for them, and re-layouts: 6.34 us -> 4.99 us
  transfers between devices with their start and end apart: 2 -> 8, of which waited for: 2 -> 7; matrix products, arithmetic and copies ran while one was open for 2% -> 9% of each run, Pallas kernels for 0% -> 0%
where the time goes in v1:
time: 147 us; the launch traced here: 146 us
  waiting for transfers between devices  72.9 us (50%)
  other arithmetic  21.9 us (15%)
  local copies, waits for them, and re-layouts  16.9 us (11%)
  between operations  14.6 us (10%)
  blocking collectives  8.28 us (6%)
  starting transfers between devices  6.63 us (5%)
  matrix products  5.03 us (3%)
    unnamed x4, waiting for transfers between devices  59.2 us
    ppermute x6, waiting for transfers between devices, collect(): theirs = lax.ppermute(grown, axis, [(d, d ^ reach) for d in range(ways)])  13.8 us
    all_gather x1, blocking collectives, local(): all_bands = lax.all_gather(flattened, 'band', axis=0, tiled=True)  8.28 us
    ppermute x6, starting transfers between devices, collect(): theirs = lax.ppermute(grown, axis, [(d, d ^ reach) for d in range(ways)])  6.37 us
    reduce_sum x2, other arithmetic, block_terms(): jnp.sum(prod_real[None] * coh_real - prod_imag[None] * coh_imag, axis=1)  6.35 us
    unnamed x23, local copies, waits for them, and re-layouts  4.99 us
    convert_element_type x1, other arithmetic, block_terms(): cohere = coh_block.astype(jnp.float32)  4.01 us
    broadcast_in_dim x4, local copies, waits for them, and re-layouts, block_terms(): left_gains = jnp.repeat(gains_first, tile_width, axis=-1)  3.11 us
  transfers between devices with their start and end apart: 8, of which 7 were waited for; matrix products, arithmetic and copies ran while one was open for 9% of the time, Pallas kernels for 0%

profile of v1, /device:TPU:0, one launch (start us, length us, event | category | flops | bytes accessed | tf_op | source)
XLA Modules:
  0.0 146.3 jit_solution(4256167113373198162)
XLA Ops:
  7.2 0.6 collective-permute-start
  7.8 1.0 slice_reduce_fusion.1
  8.7 0.9 not_reduce_fusion
  9.7 1.1 fusion.91
  10.8 0.7 iota_compare_fusion.13
  11.6 0.9 concatenate.232
  12.5 4.0 %convert_element_type.71 = f32[1,2,8,2,32,1024]{5,4,3,2,1,0:T(8,128)} convert(bf16[1,2,8,2,32,1024]{5,4,3,2,1,0:T(8,128)(2,1)} %param.8) | non-fusion elementwise | flops 1048576 | bytes 6291456 | tf_op jit(solution)/shard_map/vmap(vmap())/convert_element_type | solution.py:45
  16.7 2.6 %collective-permute-start.1 = (f32[1,2,32,128]{3,2,1,0:T(8,128)S(1)}, f32[1,2,32,128]{3,2,1,0:T(8,128)S(1)}, u32[]{:S(2)}, u32[]{:S(2)}) collective-permute-start(f32[1,2,32,128]{3,2,1,0:T(8,128)S(1)} %maximum_select_fusion.12), channel_id=1, source_target_pairs={{0,2},{1,3},{2,0},{3,1},{4,6},{5,7},{6,4},{7,5},{8,10},{9,11},{10,... | collective-permute-start | bytes 98312 | tf_op jit(solution)/shard_map/ppermute | solution.py:20
  19.7 1.7 %collective-permute-done.1 = f32[1,2,32,128]{3,2,1,0:T(8,128)S(1)} collective-permute-done((f32[1,2,32,128]{3,2,1,0:T(8,128)S(1)}, f32[1,2,32,128]{3,2,1,0:T(8,128)S(1)}, u32[]{:S(2)}, u32[]{:S(2)}) %collective-permute-start.1) | collective-permute-done | bytes 32800 | tf_op jit(solution)/shard_map/ppermute | solution.py:20
  21.4 3.0 %collective-permute-start.2 = (f32[1,2,32,256]{3,2,1,0:T(8,128)S(1)}, f32[1,2,32,256]{3,2,1,0:T(8,128)S(1)}, u32[]{:S(2)}, u32[]{:S(2)}) collective-permute-start(f32[1,2,32,256]{3,2,1,0:T(8,128)S(1)} %maximum_select_fusion.10), channel_id=1, source_target_pairs={{0,4},{1,5},{2,6},{3,7},{4,0},{5,1},{6,2},{7,3},{8,12},{9,13},{10,... | collective-permute-start | bytes 196616 | tf_op jit(solution)/shard_map/ppermute | solution.py:20
  24.7 2.4 %collective-permute-done.2 = f32[1,2,32,256]{3,2,1,0:T(8,128)S(1)} collective-permute-done((f32[1,2,32,256]{3,2,1,0:T(8,128)S(1)}, f32[1,2,32,256]{3,2,1,0:T(8,128)S(1)}, u32[]{:S(2)}, u32[]{:S(2)}) %collective-permute-start.2) | collective-permute-done | bytes 65568 | tf_op jit(solution)/shard_map/ppermute | solution.py:20
  27.5 0.6 broadcast_in_dim.9
  28.1 1.0 broadcast_in_dim.10
  29.6 1.0 tile.9
  30.6 3.2 %subtract_reduce_fusion.3 = (f32[2,8,1024]{2,1,0:T(8,128)S(1)}, f32[2,8,1024]{2,1,0:T(8,128)S(1)}) fusion(f32[1,2,8,2,32,1024]{5,4,3,2,1,0:T(8,128)} %convert_element_type.71, f32[2,32,1024]{2,1,0:T(8,128)S(1)} %get-tuple-element.26, f32[2,32,1024]{2,1,0:T(8,128)S(1)} %get-tuple-element.25), kind=kLoop, calls=%fused_computation.9 | loop fusion | flops 4161536 | bytes 4849664 | tf_op jit(solution)/shard_map/vmap(vmap())/reduce_sum | solution.py:48
  34.1 0.6 add_reduce_fusion.2
  35.0 0.7 reshape.1406
  35.7 0.6 reduce_sum.132
  36.3 0.5 fusion.39
  36.8 0.7 reshape.1407
  38.0 0.5 fusion.1
  38.8 1.0 reshape.1423
  40.3 0.7 cholesky.16
  41.0 31.5 %reduce-scatter.7.cloned.1.call-done = f32[64,64]{1,0:T(8,128)} async-done(((f32[512,64]{1,0:T(8,128)}), f32[64,64]{1,0:T(8,128)}) %reduce-scatter.7.cloned.1.call-update) | async-done | bytes 16400
  72.5 0.9 reshape.1424
  73.7 1.1 collective-permute-done.3
  75.2 3.6 %collective-permute-done.4 = f32[1,2,32,128]{3,2,1,0:T(8,128)S(1)} collective-permute-done((f32[1,2,32,128]{3,2,1,0:T(8,128)S(1)}, f32[1,2,32,128]{3,2,1,0:T(8,128)S(1)}, u32[]{:S(2)}, u32[]{:S(2)}) %collective-permute-start.4) | collective-permute-done | bytes 32800 | tf_op jit(solution)/shard_map/ppermute | solution.py:20
  79.2 5.0 %collective-permute-done.5 = f32[1,2,32,256]{3,2,1,0:T(8,128)S(1)} collective-permute-done((f32[1,2,32,256]{3,2,1,0:T(8,128)S(1)}, f32[1,2,32,256]{3,2,1,0:T(8,128)S(1)}, u32[]{:S(2)}, u32[]{:S(2)}) %collective-permute-start.5) | collective-permute-done | bytes 65568 | tf_op jit(solution)/shard_map/ppermute | solution.py:20
  85.0 0.6 broadcast_in_dim.11
  85.6 1.0 broadcast_in_dim.12
  86.7 1.0 tile.21
  87.8 3.2 %subtract_reduce_fusion.1 = (f32[2,8,1024]{2,1,0:T(8,128)S(1)}, f32[2,8,1024]{2,1,0:T(8,128)S(1)}) fusion(f32[1,2,8,2,32,1024]{5,4,3,2,1,0:T(8,128)} %convert_element_type.71, f32[2,32,1024]{2,1,0:T(8,128)S(1)} %get-tuple-element.20, f32[2,32,1024]{2,1,0:T(8,128)S(1)} %get-tuple-element.19), kind=kLoop, calls=%fused_computation.5 | loop fusion | flops 4161536 | bytes 4849664 | tf_op jit(solution)/shard_map/vmap(vmap())/reduce_sum | solution.py:48
  91.2 0.6 add_reduce_fusion
  91.9 0.9 fusion.6
  92.8 0.7 reshape.1410
  94.0 0.7 reshape.1409
  94.7 0.6 reduce_sum.142
  95.8 0.5 fusion
  96.6 1.0 reshape.1425
  97.7 0.6 compare_reduce_fusion
  98.3 0.6 fusion.49
  98.9 0.6 custom-call.10
  99.6 27.7 %reduce-scatter.9.cloned.1.call-done = f32[64,64]{1,0:T(8,128)} async-done(((f32[512,64]{1,0:T(8,128)}), f32[64,64]{1,0:T(8,128)}) %reduce-scatter.9.cloned.1.call-update) | async-done | bytes 16400
  127.2 0.9 reshape.1426
  128.2 0.6 fusion.90
  128.9 8.3 %all-gather = f32[4,1,4096]{2,1,0:T(1,128)S(1)} all-gather(f32[1,1,4096]{2,1,0:T(1,128)S(1)} %reshape.1414), channel_id=1, replica_groups=mesh['band'=4,'pair'=8] {'band'}, dimensions={0}, use_global_device_ids=true | all-gather | bytes 81920 | tf_op jit(solution)/shard_map/all_gather | solution.py:126
  137.6 0.5 fusion.22
  138.9 0.6 sub.231
  (85 shorter events, 8.8 us)
Async XLA Ops:
  7.2 65.3 %reduce-scatter.7.cloned.1.call-start = ((), (), s32[]{:S(2)}) async-start(), calls=%async_computation.2 | async-start | bytes 294912
  7.2 9.4 %collective-permute-start = (f32[1,2,32,64]{3,2,1,0:T(8,128)}, f32[1,2,32,64]{3,2,1,0:T(8,128)S(1)}, u32[]{:S(2)}, u32[]{:S(2)}) collective-permute-start(f32[1,2,32,64]{3,2,1,0:T(8,128)} %param.11), channel_id=1, source_target_pairs={{0,1},{1,0},{2,3},{3,2},{4,5},{5,4},{6,7},{7,6},{8,9},{9,8},{10,11... | collective-permute-start | bytes 49160 | tf_op jit(solution)/shard_map/ppermute | solution.py:20
  12.5 4.1 %copy-start.3 = (f32[1,2,32,64]{3,2,1,0:T(8,128)S(1)}, f32[1,2,32,64]{3,2,1,0:T(8,128)}, u32[]{:S(2)}) copy-start(f32[1,2,32,64]{3,2,1,0:T(8,128)} %param.11) | copy-start | bytes 49156
  16.7 4.7 %collective-permute-start.1 = (f32[1,2,32,128]{3,2,1,0:T(8,128)S(1)}, f32[1,2,32,128]{3,2,1,0:T(8,128)S(1)}, u32[]{:S(2)}, u32[]{:S(2)}) collective-permute-start(f32[1,2,32,128]{3,2,1,0:T(8,128)S(1)} %maximum_select_fusion.12), channel_id=1, source_target_pairs={{0,2},{1,3},{2,0},{3,1},{4,6},{5,7},{6,4},{7,5},{8,10},{9,11},{10,... | collective-permute-start | bytes 98312 | tf_op jit(solution)/shard_map/ppermute | solution.py:20
  21.4 5.6 %collective-permute-start.2 = (f32[1,2,32,256]{3,2,1,0:T(8,128)S(1)}, f32[1,2,32,256]{3,2,1,0:T(8,128)S(1)}, u32[]{:S(2)}, u32[]{:S(2)}) collective-permute-start(f32[1,2,32,256]{3,2,1,0:T(8,128)S(1)} %maximum_select_fusion.10), channel_id=1, source_target_pairs={{0,4},{1,5},{2,6},{3,7},{4,0},{5,1},{6,2},{7,3},{8,12},{9,13},{10,... | collective-permute-start | bytes 196616 | tf_op jit(solution)/shard_map/ppermute | solution.py:20
  30.6 3.5 %copy-start = (f32[1,2,8,2,32,1024]{5,4,3,2,1,0:T(8,128)S(1)}, f32[1,2,8,2,32,1024]{5,4,3,2,1,0:T(8,128)}, u32[]{:S(2)}) copy-start(f32[1,2,8,2,32,1024]{5,4,3,2,1,0:T(8,128)} %convert_element_type.71) | copy-start | bytes 12582916
  37.9 35.5 %copy-start.5 = (f32[1,2,32,64]{3,2,1,0:T(8,128)S(1)}, f32[1,2,32,64]{3,2,1,0:T(8,128)}, u32[]{:S(2)}) copy-start(f32[1,2,32,64]{3,2,1,0:T(8,128)} %param.13) | copy-start | bytes 49156
  38.0 35.5 %copy-start.6 = (f32[1,2,32,64]{3,2,1,0:T(8,128)S(1)}, f32[1,2,32,64]{3,2,1,0:T(8,128)}, u32[]{:S(2)}) copy-start(f32[1,2,32,64]{3,2,1,0:T(8,128)} %param.12) | copy-start | bytes 49156
  39.8 87.4 %reduce-scatter.9.cloned.1.call-start = ((), (), s32[]{:S(2)}) async-start(), calls=%async_computation.3 | async-start | bytes 294912
  73.5 1.3 collective-permute-start.3
  74.8 4.0 %collective-permute-start.4 = (f32[1,2,32,128]{3,2,1,0:T(8,128)S(1)}, f32[1,2,32,128]{3,2,1,0:T(8,128)S(1)}, u32[]{:S(2)}, u32[]{:S(2)}) collective-permute-start(f32[1,2,32,128]{3,2,1,0:T(8,128)S(1)} %maximum_select_fusion.14), channel_id=1, source_target_pairs={{0,2},{1,3},{2,0},{3,1},{4,6},{5,7},{6,4},{7,5},{8,10},{9,11},{10,... | collective-permute-start | bytes 98312 | tf_op jit(solution)/shard_map/ppermute | solution.py:20
  78.8 5.4 %collective-permute-start.5 = (f32[1,2,32,256]{3,2,1,0:T(8,128)S(1)}, f32[1,2,32,256]{3,2,1,0:T(8,128)S(1)}, u32[]{:S(2)}, u32[]{:S(2)}) collective-permute-start(f32[1,2,32,256]{3,2,1,0:T(8,128)S(1)} %maximum_select_fusion.11), channel_id=1, source_target_pairs={{0,4},{1,5},{2,6},{3,7},{4,0},{5,1},{6,2},{7,3},{8,12},{9,13},{10,... | collective-permute-start | bytes 196616 | tf_op jit(solution)/shard_map/ppermute | solution.py:20
  87.8 3.5 %copy-start.1 = (f32[1,2,8,2,32,1024]{5,4,3,2,1,0:T(8,128)S(1)}, f32[1,2,8,2,32,1024]{5,4,3,2,1,0:T(8,128)}, u32[]{:S(2)}) copy-start(f32[1,2,8,2,32,1024]{5,4,3,2,1,0:T(8,128)} %convert_element_type.71) | copy-start | bytes 12582916
  92.8 1.2 copy-start.2
  138.8 0.6 copy-start.4
Sparse Core Ops, SparseCore 0:
  40.0 32.4 reduce-scatter.6
  97.8 29.4 reduce-scatter.8
